TPU v7x, 32 devices: a whole 2x2x4 slice. The times are simulated.
32 devices in a mesh: grp: 4 (over y, x), row: 2 (over core), col: 4 (over z).
Axes of the slice: x: 2, y: 2, z: 4, core: 2. Of those that a mesh axis runs over, the one named last changes fastest.
Arguments:
- normals: float32 [4, 4096, 4096], P('grp', 'row', 'col'), as said below
- transforms: float32 [4, 32, 128, 128], P('grp', 'row'), as said below
- block_map: int32 [4, 32], P('grp'), may hold values from 0 to 31, as said below
Outputs:
- eliminated: float32 [4096, 4096], P('row', 'col')
Inputs may be any that keep to these rules, and one draw needn't show every extreme that they name: `block_map`: for each group, a permutation of the blocks that maps every aligned range of 8 blocks onto itself. `normals`: each group's matrix is symmetric positive definite. `transforms`: each block is nonsingular.
All inputs are finite; a program needn't handle non-finite values.
Results may differ from a plain program's by a relative error of at most 0.0001.
Values sent between devices are 32-bit elements; how exact they have to be, the bound alone decides.
No kernel may reach another device: no remote copies, remote signals or barrier semaphores. Data moves between devices by JAX's collectives and lax.ppermute only.
A program may use at most 64 MiB of HBM per device.

v0:
```python
import jax
import jax.numpy as jnp
from jax import lax
from jax.sharding import PartitionSpec as P

BLK = 128
NPAN = 5


def spread(block, axis, holder):
    block = jnp.where(lax.axis_index(axis) == holder, block, jnp.zeros_like(block))
    return lax.psum(block, axis)


def on_device(normals, transforms, block_map):
    local = normals[0]
    height, width = local.shape
    row_blocks = height // BLK
    col_blocks = width // BLK
    row_index = lax.axis_index("row")
    col_index = lax.axis_index("col")
    row_transforms = transforms[0]
    every_block = lax.all_gather(transforms, "row", axis=1, tiled=True)[0]
    col_transforms = lax.dynamic_slice_in_dim(every_block, col_index * col_blocks, col_blocks, 0)
    grid = local.reshape(row_blocks, BLK, col_blocks, BLK)
    half_done = jnp.einsum("aij,aibk->ajbk", row_transforms, grid, precision=lax.Precision.HIGHEST)
    rotated = jnp.einsum(
        "ajbk,bkl->ajbl", half_done, col_transforms, precision=lax.Precision.HIGHEST
    )
    mapping = block_map[0]
    row_map = (
        lax.dynamic_slice_in_dim(mapping, row_index * row_blocks, row_blocks, 0)
        - row_index * row_blocks
    )
    col_map = (
        lax.dynamic_slice_in_dim(mapping, col_index * col_blocks, col_blocks, 0)
        - col_index * col_blocks
    )
    rotated = jnp.take(rotated, row_map, axis=0)
    rotated = jnp.take(rotated, col_map, axis=2).reshape(height, width)
    matrix = lax.psum(rotated, "grp")
    row_offset = row_index * height
    own_count = matrix.shape[0]
    order_all = height * lax.axis_size("row")
    col_offset = col_index * width
    for panel in range(NPAN):
        offset = panel * BLK
        holder = offset // width
        inside = offset - holder * width
        panel_piece = spread(matrix[:, inside : inside + BLK], "col", holder)
        column = lax.all_gather(panel_piece, "row", axis=0, tiled=True)
        factor_block = jnp.linalg.cholesky(column[offset : offset + BLK])
        factor = lax.linalg.triangular_solve(
            factor_block, column, left_side=False, lower=True, transpose_a=True
        )
        below = jnp.arange(order_all)[:, None] >= offset
        factor = jnp.where(below, factor, jnp.zeros_like(factor))
        own_rows = lax.dynamic_slice_in_dim(factor, row_offset, own_count, 0)
        col_rows = lax.dynamic_slice_in_dim(factor, col_offset, width, 0)
        matrix = matrix - jnp.dot(
            own_rows,
            col_rows.T,
            precision=lax.Precision.HIGHEST,
            preferred_element_type=jnp.float32,
        )
        current = matrix[:, inside : inside + BLK]
        matrix = matrix.at[:, inside : inside + BLK].set(
            jnp.where(col_index == holder, own_rows, current)
        )
    return matrix


def solution(mesh):
    return jax.shard_map(
        on_device,
        mesh=mesh,
        in_specs=(P("grp", "row", "col"), P("grp", "row", None, None), P("grp", None)),
        out_specs=P("row", "col"),
        check_vma=False,
    )
```

profile of v0, /device:TPU:0, one launch (start us, length us, event | category | flops | bytes accessed | tf_op | source)
XLA Modules:
  0.0 811.8 jit_solution(7198959561113941672)
XLA Ops:
  16.7 14.3 %fusion = f32[16,128,8,128]{3,1,0,2:T(8,128)} fusion(f32[16,128,8,128]{3,2,1,0:T(8,128)} %bitcast.108, f32[1,16,128,128]{3,2,1,0:T(8,128)S(1)} %copy-done.4), kind=kOutput, calls=%fused_computation.3 | convolution fusion | flops 3221225472 | bytes 17825792 | tf_op jit(solution)/shard_map/aij,aibk->ajbk/dot_general | solution.py:26
  31.0 12.0 %convolution_bitcast_fusion.5 = f32[16,128,8,128]{1,3,0,2:T(8,128)} fusion(f32[16,128,8,128]{3,1,0,2:T(8,128)} %fusion, f32[1,32,128,128]{3,2,0,1:T(8,128)} %all-gather.7.cloned.1.call-done, s32[]{:T(128)S(6)} %select_n.123), kind=kOutput, calls=%fused_computation.20 | convolution fusion | flops 3221225472 | bytes 17301508 | tf_op jit(solution)/shard_map/ajbk,bkl->ajbl/dot_general | solution.py:27
  82.2 174.8 %all-reduce.7.cloned.1.call-done = f32[2048,1024]{0,1:T(8,128)} async-done(((f32[2048,1024]{0,1:T(8,128)}), f32[2048,1024]{0,1:T(8,128)}) %all-reduce.7.cloned.1.call-update) | async-done | bytes 8388624 | tf_op jit(solution)/shard_map/psum | solution.py:41
  259.4 52.7 %all-reduce.9.cloned.1.call-done = f32[2048,128]{0,1:T(8,128)} async-done(((f32[2048,128]{0,1:T(8,128)}), f32[2048,128]{0,1:T(8,128)}) %all-reduce.9.cloned.1.call-update) | async-done | bytes 1048592 | tf_op jit(solution)/shard_map/psum | solution.py:12
  313.0 10.3 %all-gather.9.cloned.1.call-done = f32[4096,128]{0,1:T(8,128)} async-done(((f32[2048,128]{0,1:T(8,128)}), f32[4096,128]{0,1:T(8,128)}) %all-gather.9.cloned.1.call-update) | async-done | bytes 2097168 | tf_op jit(solution)/shard_map/all_gather | solution.py:51
  325.1 11.7 %cholesky.89 = f32[128,128]{1,0:T(8,128)S(1)} custom-call(f32[128,128]{1,0:T(8,128)S(1)} %fusion.38), custom_call_target="Cholesky" | custom-call | tf_op jit(solution)/shard_map/jit(cholesky)/cholesky | solution.py:52
  338.2 9.8 %custom-call.9 = f32[1,128,128]{1,2,0:T(8,128)S(1)} custom-call(f32[1,128,128]{2,1,0:T(8,128)S(1)} %fusion.24), custom_call_target="InvertDiagBlocksLowerTriangular" | custom-call | tf_op jit(solution)/shard_map/triangular_solve/custom-call.0 | solution.py:53
  366.4 53.2 %all-reduce.11.cloned.1.call-done = f32[2048,128]{0,1:T(8,128)} async-done(((f32[2048,128]{0,1:T(8,128)}), f32[2048,128]{0,1:T(8,128)}) %all-reduce.11.cloned.1.call-update) | async-done | bytes 1048592 | tf_op jit(solution)/shard_map/psum | solution.py:12
  420.7 10.1 %all-gather.11.cloned.1.call-done = f32[4096,128]{0,1:T(8,128)} async-done(((f32[2048,128]{0,1:T(8,128)}), f32[4096,128]{0,1:T(8,128)}) %all-gather.11.cloned.1.call-update) | async-done | bytes 2097168 | tf_op jit(solution)/shard_map/all_gather | solution.py:51
  432.6 11.7 %cholesky.100 = f32[128,128]{1,0:T(8,128)S(1)} custom-call(f32[128,128]{1,0:T(8,128)S(1)} %fusion.36), custom_call_target="Cholesky" | custom-call | tf_op jit(solution)/shard_map/jit(cholesky)/cholesky | solution.py:52
  445.7 9.8 %custom-call.10 = f32[1,128,128]{1,2,0:T(8,128)S(1)} custom-call(f32[1,128,128]{2,1,0:T(8,128)S(1)} %fusion.25), custom_call_target="InvertDiagBlocksLowerTriangular" | custom-call | tf_op jit(solution)/shard_map/triangular_solve/custom-call.0 | solution.py:53
  473.8 53.2 %all-reduce.13.cloned.1.call-done = f32[2048,128]{0,1:T(8,128)} async-done(((f32[2048,128]{0,1:T(8,128)}), f32[2048,128]{0,1:T(8,128)}) %all-reduce.13.cloned.1.call-update) | async-done | bytes 1048592 | tf_op jit(solution)/shard_map/psum | solution.py:12
  527.9 10.6 %all-gather.13.cloned.1.call-done = f32[4096,128]{0,1:T(8,128)} async-done(((f32[2048,128]{0,1:T(8,128)}), f32[4096,128]{0,1:T(8,128)}) %all-gather.13.cloned.1.call-update) | async-done | bytes 2097168 | tf_op jit(solution)/shard_map/all_gather | solution.py:51
  540.2 11.7 %cholesky.111 = f32[128,128]{1,0:T(8,128)S(1)} custom-call(f32[128,128]{1,0:T(8,128)S(1)} %fusion.34), custom_call_target="Cholesky" | custom-call | tf_op jit(solution)/shard_map/jit(cholesky)/cholesky | solution.py:52
  553.2 9.8 %custom-call.11 = f32[1,128,128]{1,2,0:T(8,128)S(1)} custom-call(f32[1,128,128]{2,1,0:T(8,128)S(1)} %fusion.26), custom_call_target="InvertDiagBlocksLowerTriangular" | custom-call | tf_op jit(solution)/shard_map/triangular_solve/custom-call.0 | solution.py:53
  581.8 52.8 %all-reduce.15.cloned.1.call-done = f32[2048,128]{0,1:T(8,128)} async-done(((f32[2048,128]{0,1:T(8,128)}), f32[2048,128]{0,1:T(8,128)}) %all-reduce.15.cloned.1.call-update) | async-done | bytes 1048592 | tf_op jit(solution)/shard_map/psum | solution.py:12
  635.3 10.6 %all-gather.15.cloned.1.call-done = f32[4096,128]{0,1:T(8,128)} async-done(((f32[2048,128]{0,1:T(8,128)}), f32[4096,128]{0,1:T(8,128)}) %all-gather.15.cloned.1.call-update) | async-done | bytes 2097168 | tf_op jit(solution)/shard_map/all_gather | solution.py:51
  647.6 11.7 %cholesky.122 = f32[128,128]{1,0:T(8,128)S(1)} custom-call(f32[128,128]{1,0:T(8,128)S(1)} %fusion.32), custom_call_target="Cholesky" | custom-call | tf_op jit(solution)/shard_map/jit(cholesky)/cholesky | solution.py:52
  660.7 9.8 %custom-call.12 = f32[1,128,128]{1,2,0:T(8,128)S(1)} custom-call(f32[1,128,128]{2,1,0:T(8,128)S(1)} %fusion.27), custom_call_target="InvertDiagBlocksLowerTriangular" | custom-call | tf_op jit(solution)/shard_map/triangular_solve/custom-call.0 | solution.py:53
  689.0 53.0 %all-reduce.17.cloned.1.call-done = f32[2048,128]{0,1:T(8,128)} async-done(((f32[2048,128]{0,1:T(8,128)}), f32[2048,128]{0,1:T(8,128)}) %all-reduce.17.cloned.1.call-update) | async-done | bytes 1048592 | tf_op jit(solution)/shard_map/psum | solution.py:12
  742.7 10.6 %all-gather.17.cloned.1.call-done = f32[4096,128]{0,1:T(8,128)} async-done(((f32[2048,128]{0,1:T(8,128)}), f32[4096,128]{0,1:T(8,128)}) %all-gather.17.cloned.1.call-update) | async-done | bytes 2097168 | tf_op jit(solution)/shard_map/all_gather | solution.py:51
  755.1 11.7 %cholesky.133 = f32[128,128]{1,0:T(8,128)S(1)} custom-call(f32[128,128]{1,0:T(8,128)S(1)} %fusion.30), custom_call_target="Cholesky" | custom-call | tf_op jit(solution)/shard_map/jit(cholesky)/cholesky | solution.py:52
  768.1 9.8 %custom-call.13 = f32[1,128,128]{1,2,0:T(8,128)S(1)} custom-call(f32[1,128,128]{2,1,0:T(8,128)S(1)} %fusion.28), custom_call_target="InvertDiagBlocksLowerTriangular" | custom-call | tf_op jit(solution)/shard_map/triangular_solve/custom-call.0 | solution.py:53
  781.5 11.2 %convolution_subtract_fusion = f32[2048,1024]{0,1:T(8,128)} fusion(f32[2048,1024]{0,1:T(8,128)} %copy-done.3, f32[4096,128]{0,1:T(8,128)S(1)} %fusion.2, s32[]{:T(128)S(6)} %select_n.133, s32[]{:T(128)S(6)} %select_n.134), kind=kOutput, calls=%fused_computation.14 | convolution fusion | flops 3223322624 | bytes 18350088 | tf_op jit(solution)/shard_map/dot_general | solution.py:60
  (109 shorter events, 160.8 us)
Async XLA Ops:
  6.5 24.5 %all-gather.7.cloned.1.call-start = ((), (), s32[]{:S(2)}) async-start(), calls=%async_computation | async-start | bytes 3145728 | tf_op jit(solution)/shard_map/all_gather | solution.py:23
  7.3 249.7 %all-reduce.7.cloned.1.call-start = ((), (), s32[]{:S(2)}) async-start(), calls=%async_computation.1 | async-start | bytes 16777216 | tf_op jit(solution)/shard_map/psum | solution.py:41
  7.3 9.0 %copy-start.5 = (s32[1,32]{1,0:T(1,128)S(1)}, s32[1,32]{1,0:T(1,128)}, u32[]{:S(2)}) copy-start(s32[1,32]{1,0:T(1,128)} %param.18) | copy-start | bytes 388
  7.3 9.4 %copy-start.4 = (f32[1,16,128,128]{3,2,1,0:T(8,128)S(1)}, f32[1,16,128,128]{3,2,1,0:T(8,128)}, u32[]{:S(2)}) copy-start(f32[1,16,128,128]{3,2,1,0:T(8,128)} %param.17) | copy-start | bytes 3145732
  82.1 229.9 %all-reduce.9.cloned.1.call-start = ((), (), s32[]{:S(2)}) async-start(), calls=%async_computation.2 | async-start | bytes 2097152 | tf_op jit(solution)/shard_map/psum | solution.py:12
  259.3 64.0 %all-gather.9.cloned.1.call-start = ((), (), s32[]{:S(2)}) async-start(), calls=%async_computation.3 | async-start | bytes 3145728 | tf_op jit(solution)/shard_map/all_gather | solution.py:51
  312.1 107.5 %all-reduce.11.cloned.1.call-start = ((), (), s32[]{:S(2)}) async-start(), calls=%async_computation.4 | async-start | bytes 2097152 | tf_op jit(solution)/shard_map/psum | solution.py:12
  361.8 3.4 copy-start
  366.3 64.5 %all-gather.11.cloned.1.call-start = ((), (), s32[]{:S(2)}) async-start(), calls=%async_computation.5 | async-start | bytes 3145728 | tf_op jit(solution)/shard_map/all_gather | solution.py:51
  419.6 107.4 %all-reduce.13.cloned.1.call-start = ((), (), s32[]{:S(2)}) async-start(), calls=%async_computation.6 | async-start | bytes 2097152 | tf_op jit(solution)/shard_map/psum | solution.py:12
  469.3 3.4 copy-start.1
  473.8 64.6 %all-gather.13.cloned.1.call-start = ((), (), s32[]{:S(2)}) async-start(), calls=%async_computation.7 | async-start | bytes 3145728 | tf_op jit(solution)/shard_map/all_gather | solution.py:51
  527.0 107.6 %all-reduce.15.cloned.1.call-start = ((), (), s32[]{:S(2)}) async-start(), calls=%async_computation.8 | async-start | bytes 2097152 | tf_op jit(solution)/shard_map/psum | solution.py:12
  576.9 3.4 copy-start.2
  581.3 64.5 %all-gather.15.cloned.1.call-start = ((), (), s32[]{:S(2)}) async-start(), calls=%async_computation.9 | async-start | bytes 3145728 | tf_op jit(solution)/shard_map/all_gather | solution.py:51
  634.6 107.4 %all-reduce.17.cloned.1.call-start = ((), (), s32[]{:S(2)}) async-start(), calls=%async_computation.10 | async-start | bytes 2097152 | tf_op jit(solution)/shard_map/psum | solution.py:12
  684.3 3.4 copy-start.3
  688.8 64.5 %all-gather.17.cloned.1.call-start = ((), (), s32[]{:S(2)}) async-start(), calls=%async_computation.11 | async-start | bytes 3145728 | tf_op jit(solution)/shard_map/all_gather | solution.py:51
Sparse Core Ops, SparseCore 0:
  8.9 13.3 all-gather.6
  82.2 174.7 all-reduce.6
  259.4 52.5 all-reduce.8
  313.4 9.8 all-gather.8
  366.5 53.0 all-reduce.10
  421.0 9.8 all-gather.10
  473.9 53.0 all-reduce.12
  528.5 9.8 all-gather.12
  581.5 53.0 all-reduce.14
  636.0 9.8 all-gather.14
  688.9 53.0 all-reduce.16
  743.4 9.8 all-gather.16
where the time goes:
time: 821 us; the launch traced here: 812 us
  waiting for transfers between devices  493 us (60%)
  other arithmetic  151 us (18%)
  matrix products  92.7 us (11%)
  local copies, waits for them, and re-layouts  60 us (7%)
  between operations  14.1 us (2%)
    psum x5, waiting for transfers between devices, spread(): return lax.psum(block, axis)  265 us
    psum x1, waiting for transfers between devices, on_device(): matrix = lax.psum(rotated, 'grp')  175 us
    another operation x15, other arithmetic, on_device(): factor_block = jnp.linalg.cholesky(column[offset:offset + BLK])  62 us
    another operation x10, other arithmetic, on_device(): lax.linalg.triangular_solve(factor_block, column, left_side=False, lower=...  52.2 us
    all_gather x5, waiting for transfers between devices, on_device(): column = lax.all_gather(panel_piece, 'row', axis=0, tiled=True)  52.2 us
    dot_general x5, matrix products, on_device(): jnp.dot(own_rows, col_rows.T, precision=lax.Precision.HIGHEST, preferred_...  48.8 us
    unnamed x13, local copies, waits for them, and re-layouts  22.5 us
    another operation x5, matrix products, on_device(): lax.linalg.triangular_solve(factor_block, column, left_side=False, lower=...  17.5 us
  transfers between devices with their start and end apart: 12, of which 11 were waited for; matrix products, arithmetic and copies ran while one was open for 3% of the time, Pallas kernels for 0%

commit v1 on v0

--- a/solution.py
+++ b/solution.py
@@ -9,7 +9,7 @@
 
 def spread(block, axis, holder):
     block = jnp.where(lax.axis_index(axis) == holder, block, jnp.zeros_like(block))
-    return lax.psum(block, axis)
+    return jnp.sum(lax.all_gather(block, axis), axis=0)
 
 
 def on_device(normals, transforms, block_map):

time: 821 us -> 1020 us (1.24)
  waiting for transfers between devices: 493 us -> 627 us
  local copies, waits for them, and re-layouts: 60 us -> 90.1 us
  other arithmetic: 151 us -> 180 us
    all_gather x0 -> x5, waiting for transfers between devices: none -> 409 us  [spread(): return jnp.sum(lax.all_gather(block, axis), axis=0)]
    psum x5 -> x0, waiting for transfers between devices: 265 us -> none  [spread(): return lax.psum(block, axis)]
    all_gather x0 -> x5, local copies, waits for them, and re-layouts: none -> 30.1 us  [spread(): return jnp.sum(lax.all_gather(block, axis), axis=0)]
    reduce_sum x0 -> x5, other arithmetic: none -> 29.1 us  [spread(): return jnp.sum(lax.all_gather(block, axis), axis=0)]
where the time goes in v1:
time: 1020 us; the launch traced here: 1010 us
  waiting for transfers between devices  627 us (61%)
  other arithmetic  180 us (18%)
  matrix products  92.9 us (9%)
  local copies, waits for them, and re-layouts  90.1 us (9%)
  between operations  14.4 us (1%)
    all_gather x5, waiting for transfers between devices, spread(): return jnp.sum(lax.all_gather(block, axis), axis=0)  409 us
    psum x1, waiting for transfers between devices, on_device(): matrix = lax.psum(rotated, 'grp')  175 us
    another operation x15, other arithmetic, on_device(): factor_block = jnp.linalg.cholesky(column[offset:offset + BLK])  62 us
    another operation x10, other arithmetic, on_device(): lax.linalg.triangular_solve(factor_block, column, left_side=False, lower=...  52.2 us
    dot_general x5, matrix products, on_device(): jnp.dot(own_rows, col_rows.T, precision=lax.Precision.HIGHEST, preferred_...  49.1 us
    all_gather x5, waiting for transfers between devices, on_device(): column = lax.all_gather(panel_piece, 'row', axis=0, tiled=True)  42.3 us
    all_gather x5, local copies, waits for them, and re-layouts, spread(): return jnp.sum(lax.all_gather(block, axis), axis=0)  30.1 us
    reduce_sum x5, other arithmetic, spread(): return jnp.sum(lax.all_gather(block, axis), axis=0)  29.1 us
  transfers between devices with their start and end apart: 12, of which 11 were waited for; matrix products, arithmetic and copies ran while one was open for 3% of the time, Pallas kernels for 0%

profile of v1, /device:TPU:0, one launch (start us, length us, event | category | flops | bytes accessed | tf_op | source)
XLA Modules:
  0.0 1005.4 jit_solution(16461352752981952374)
XLA Ops:
  16.7 14.3 %fusion = f32[16,128,8,128]{3,1,0,2:T(8,128)} fusion(f32[16,128,8,128]{3,2,1,0:T(8,128)} %bitcast.119, f32[1,16,128,128]{3,2,1,0:T(8,128)S(1)} %copy-done.4), kind=kOutput, calls=%fused_computation.3 | convolution fusion | flops 3221225472 | bytes 17825792 | tf_op jit(solution)/shard_map/aij,aibk->ajbk/dot_general | solution.py:26
  31.0 12.0 %convolution_bitcast_fusion.5 = f32[16,128,8,128]{1,3,0,2:T(8,128)} fusion(f32[16,128,8,128]{3,1,0,2:T(8,128)} %fusion, f32[1,32,128,128]{3,2,0,1:T(8,128)} %all-gather.17.cloned.1.call-done, s32[]{:T(128)S(6)} %select_n.123), kind=kOutput, calls=%fused_computation.20 | convolution fusion | flops 3221225472 | bytes 17301508 | tf_op jit(solution)/shard_map/ajbk,bkl->ajbl/dot_general | solution.py:27
  82.2 174.8 %all-reduce.2.cloned.1.call-done = f32[2048,1024]{0,1:T(8,128)} async-done(((f32[2048,1024]{0,1:T(8,128)}), f32[2048,1024]{0,1:T(8,128)}) %all-reduce.2.cloned.1.call-update) | async-done | bytes 8388624 | tf_op jit(solution)/shard_map/psum | solution.py:41
  259.4 81.5 %all-gather.29.cloned.1.call-done = f32[8192,128]{0,1:T(8,128)} async-done(((f32[2048,128]{0,1:T(8,128)}), f32[8192,128]{0,1:T(8,128)}) %all-gather.29.cloned.1.call-update) | async-done | bytes 4194320 | tf_op jit(solution)/shard_map/all_gather | solution.py:12
  363.8 11.7 %cholesky.89 = f32[128,128]{1,0:T(8,128)S(1)} custom-call(f32[128,128]{1,0:T(8,128)S(1)} %fusion.38), custom_call_target="Cholesky" | custom-call | tf_op jit(solution)/shard_map/jit(cholesky)/cholesky | solution.py:52
  376.8 9.8 custom-call.9
  390.2 9.4 convolution_subtract_fusion.4
  405.2 81.8 %all-gather.31.cloned.1.call-done = f32[8192,128]{0,1:T(8,128)} async-done(((f32[2048,128]{0,1:T(8,128)}), f32[8192,128]{0,1:T(8,128)}) %all-gather.31.cloned.1.call-update) | async-done | bytes 4194320 | tf_op jit(solution)/shard_map/all_gather | solution.py:12
  509.9 11.7 %cholesky.100 = f32[128,128]{1,0:T(8,128)S(1)} custom-call(f32[128,128]{1,0:T(8,128)S(1)} %fusion.36), custom_call_target="Cholesky" | custom-call | tf_op jit(solution)/shard_map/jit(cholesky)/cholesky | solution.py:52
  523.0 9.8 custom-call.10
  536.3 9.4 convolution_subtract_fusion.3
  551.5 81.6 %all-gather.33.cloned.1.call-done = f32[8192,128]{0,1:T(8,128)} async-done(((f32[2048,128]{0,1:T(8,128)}), f32[8192,128]{0,1:T(8,128)}) %all-gather.33.cloned.1.call-update) | async-done | bytes 4194320 | tf_op jit(solution)/shard_map/all_gather | solution.py:12
  656.0 11.7 %cholesky.111 = f32[128,128]{1,0:T(8,128)S(1)} custom-call(f32[128,128]{1,0:T(8,128)S(1)} %fusion.34), custom_call_target="Cholesky" | custom-call | tf_op jit(solution)/shard_map/jit(cholesky)/cholesky | solution.py:52
  669.0 9.8 custom-call.11
  682.4 9.4 convolution_subtract_fusion.2
  697.4 81.8 %all-gather.35.cloned.1.call-done = f32[8192,128]{0,1:T(8,128)} async-done(((f32[2048,128]{0,1:T(8,128)}), f32[8192,128]{0,1:T(8,128)}) %all-gather.35.cloned.1.call-update) | async-done | bytes 4194320 | tf_op jit(solution)/shard_map/all_gather | solution.py:12
  802.1 11.7 %cholesky.122 = f32[128,128]{1,0:T(8,128)S(1)} custom-call(f32[128,128]{1,0:T(8,128)S(1)} %fusion.32), custom_call_target="Cholesky" | custom-call | tf_op jit(solution)/shard_map/jit(cholesky)/cholesky | solution.py:52
  815.1 9.8 custom-call.12
  828.4 9.4 convolution_subtract_fusion.1
  843.5 81.8 %all-gather.37.cloned.1.call-done = f32[8192,128]{0,1:T(8,128)} async-done(((f32[2048,128]{0,1:T(8,128)}), f32[8192,128]{0,1:T(8,128)}) %all-gather.37.cloned.1.call-update) | async-done | bytes 4194320 | tf_op jit(solution)/shard_map/all_gather | solution.py:12
  948.2 11.7 %cholesky.133 = f32[128,128]{1,0:T(8,128)S(1)} custom-call(f32[128,128]{1,0:T(8,128)S(1)} %fusion.30), custom_call_target="Cholesky" | custom-call | tf_op jit(solution)/shard_map/jit(cholesky)/cholesky | solution.py:52
  961.2 9.8 custom-call.13
  974.5 11.4 %convolution_subtract_fusion = f32[2048,1024]{0,1:T(8,128)} fusion(f32[2048,1024]{0,1:T(8,128)} %copy-done.3, f32[4096,128]{0,1:T(8,128)S(1)} %fusion.2, s32[]{:T(128)S(6)} %select_n.133, s32[]{:T(128)S(6)} %select_n.134), kind=kOutput, calls=%fused_computation.14 | convolution fusion | flops 3223322624 | bytes 18350088 | tf_op jit(solution)/shard_map/dot_general | solution.py:60
  988.9 9.2 copy.46
  (119 shorter events, 215.3 us)
Async XLA Ops:
  6.5 24.5 %all-gather.17.cloned.1.call-start = ((), (), s32[]{:S(2)}) async-start(), calls=%async_computation | async-start | bytes 3145728 | tf_op jit(solution)/shard_map/all_gather | solution.py:23
  7.3 249.8 %all-reduce.2.cloned.1.call-start = ((), (), s32[]{:S(2)}) async-start(), calls=%async_computation.1 | async-start | bytes 16777216 | tf_op jit(solution)/shard_map/psum | solution.py:41
  7.3 9.0 copy-start.5
  7.3 9.4 copy-start.4
  82.1 258.8 %all-gather.29.cloned.1.call-start = ((), (), s32[]{:S(2)}) async-start(), calls=%async_computation.7 | async-start | bytes 5242880 | tf_op jit(solution)/shard_map/all_gather | solution.py:12
  259.3 102.7 %all-gather.19.cloned.1.call-start = ((), (), s32[]{:S(2)}) async-start(), calls=%async_computation.2 | async-start | bytes 3145728 | tf_op jit(solution)/shard_map/all_gather | solution.py:51
  352.8 134.3 %all-gather.31.cloned.1.call-start = ((), (), s32[]{:S(2)}) async-start(), calls=%async_computation.8 | async-start | bytes 5242880 | tf_op jit(solution)/shard_map/all_gather | solution.py:12
  400.5 3.4 copy-start
  405.0 103.1 %all-gather.21.cloned.1.call-start = ((), (), s32[]{:S(2)}) async-start(), calls=%async_computation.3 | async-start | bytes 3145728 | tf_op jit(solution)/shard_map/all_gather | solution.py:51
  498.9 134.2 %all-gather.33.cloned.1.call-start = ((), (), s32[]{:S(2)}) async-start(), calls=%async_computation.9 | async-start | bytes 5242880 | tf_op jit(solution)/shard_map/all_gather | solution.py:12
  546.6 3.4 copy-start.1
  551.1 103.2 %all-gather.23.cloned.1.call-start = ((), (), s32[]{:S(2)}) async-start(), calls=%async_computation.4 | async-start | bytes 3145728 | tf_op jit(solution)/shard_map/all_gather | solution.py:51
  645.0 134.2 %all-gather.35.cloned.1.call-start = ((), (), s32[]{:S(2)}) async-start(), calls=%async_computation.10 | async-start | bytes 5242880 | tf_op jit(solution)/shard_map/all_gather | solution.py:12
  692.7 3.4 copy-start.2
  697.1 103.1 %all-gather.25.cloned.1.call-start = ((), (), s32[]{:S(2)}) async-start(), calls=%async_computation.5 | async-start | bytes 3145728 | tf_op jit(solution)/shard_map/all_gather | solution.py:51
  791.1 134.2 %all-gather.37.cloned.1.call-start = ((), (), s32[]{:S(2)}) async-start(), calls=%async_computation.11 | async-start | bytes 5242880 | tf_op jit(solution)/shard_map/all_gather | solution.py:12
  838.7 3.4 copy-start.3
  843.2 103.2 %all-gather.27.cloned.1.call-start = ((), (), s32[]{:S(2)}) async-start(), calls=%async_computation.6 | async-start | bytes 3145728 | tf_op jit(solution)/shard_map/all_gather | solution.py:51
Sparse Core Ops, SparseCore 0:
  8.9 13.3 all-gather.16
  82.3 174.7 all-reduce.1
  259.4 81.4 all-gather.28
  352.9 9.0 all-gather.18
  405.1 81.8 all-gather.30
  499.0 9.0 all-gather.20
  551.2 81.9 all-gather.32
  645.1 9.0 all-gather.22
  697.3 81.8 all-gather.34
  791.2 9.0 all-gather.24
  843.3 81.8 all-gather.36
  937.3 9.0 all-gather.26
